TPU v7x, 32 devices: a whole 2x2x4 slice. The times are simulated.
32 devices in a mesh: group: 2 (over x), expert: 16 (over z, y, core).
Axes of the slice: x: 2, y: 2, z: 4, core: 2. Of those that a mesh axis runs over, the one named last changes fastest.
Arguments:
- tokens: bfloat16 [128, 7168], P(('group', 'expert')), parts along dimension 0, may hold values from -6 to 6
- expert_ids: int32 [128, 2], P(('group', 'expert')), parts along dimension 0, may hold values from 0 to 1, all different within a row; in each aligned block of 4 rows (0 to 3, 4 to 7, ...) at most 4 rows name the same one
- gate_codes: int32 [128, 2], P(('group', 'expert')), parts along dimension 0, may hold values from 1 to 65535
- gate_weight: bfloat16 [16, 7168, 256], P('expert'), may hold values from -0.0625 to 0.0625
- up_weight: bfloat16 [16, 7168, 256], P('expert'), may hold values from -0.0625 to 0.0625
- down_weight: bfloat16 [16, 256, 7168], P('expert'), may hold values from -0.125 to 0.125
- target_basis: bfloat16 [7168, 512], P('expert'), may hold values from -0.0625 to 0.0625
Outputs:
- targets: bfloat16 [128, 512], P(('group', 'expert')), parts along dimension 0
There are 2 independent parts, one for each index of `group`. A program takes and returns all parts, laid end to end along the dimension named above; an argument that names none is the same for every part. Nothing has to cross between parts.
Inputs may be any that keep to these rules, and one draw needn't show every extreme that they name: `expert_ids`: each row names 2 different experts; among the 4 rows of one device no expert is named more than 4 times, a bound that some block reaches.
All inputs are finite; a program needn't handle non-finite values.
Results may differ from a plain program's by a relative error of at most 0.0057.
Values may be sent and summed in bfloat16 or wider, within the bound.
No kernel may reach another device: no remote copies, remote signals or barrier semaphores. Data moves between devices by JAX's collectives and lax.ppermute only.
A program may use at most 128 MiB of HBM per device.

v0:
```python
import jax
import jax.numpy as jnp
from jax import lax
from jax.sharding import PartitionSpec as P

SLICES = 8


def run_expert(received, gate_weight, up_weight, down_weight):
    sources, slots, feature_width = received.shape
    row_block = received.reshape(sources * slots, feature_width)
    gate_act = jnp.dot(row_block, gate_weight[0], preferred_element_type=jnp.float32)
    up_act = jnp.dot(row_block, up_weight[0], preferred_element_type=jnp.float32)
    hidden = (jax.nn.silu(gate_act) * up_act).astype(jnp.bfloat16)
    expert_part = jnp.dot(hidden, down_weight[0], preferred_element_type=jnp.float32).astype(
        jnp.bfloat16
    )
    return expert_part.reshape(sources, slots, feature_width)


def shards(tokens, expert_ids, gate_codes, gate_weight, up_weight, down_weight, target_basis):
    token_count, feature_width = tokens.shape
    pick_count = expert_ids.shape[1]
    owner_count = lax.axis_size("expert")
    expert_count = owner_count // SLICES
    capacity = min(token_count, max(2, 5 * token_count * pick_count // (4 * expert_count)))
    rank_width = target_basis.shape[1]
    flat_ids = expert_ids.reshape(-1)
    onehot = (flat_ids[:, None] == jnp.arange(expert_count, dtype=jnp.int32)[None, :]).astype(
        jnp.int32
    )
    before = jnp.cumsum(onehot, axis=0) - onehot
    slot_rank = jnp.sum(before * onehot, axis=1)
    slot_index = flat_ids * capacity + slot_rank
    row_token = jnp.arange(token_count * pick_count, dtype=jnp.int32) // pick_count
    slot_table = (
        jnp.full((expert_count * capacity,), token_count, jnp.int32).at[slot_index].set(row_token)
    )
    padded = jnp.concatenate([tokens, jnp.zeros((1, feature_width), tokens.dtype)], axis=0)
    per_expert_rows = padded[slot_table].reshape(expert_count, 1, capacity, feature_width)
    outgoing = jnp.broadcast_to(per_expert_rows, (expert_count, SLICES, capacity, feature_width))
    outgoing = outgoing.reshape(owner_count, capacity, feature_width)
    full_basis = lax.all_gather(target_basis, "expert", axis=0, tiled=True)
    expert_part = run_expert(
        lax.all_to_all(outgoing, "expert", split_axis=0, concat_axis=0, tiled=True),
        gate_weight,
        up_weight,
        down_weight,
    )
    result = jnp.einsum("skd,dr->skr", expert_part, full_basis, preferred_element_type=jnp.float32)
    returned = lax.all_to_all(result, "expert", split_axis=0, concat_axis=0, tiled=True)
    summed = jnp.sum(returned.reshape(expert_count, SLICES, capacity, rank_width), axis=1)
    projected = summed.reshape(expert_count * capacity, rank_width)[slot_index]
    codes_float = gate_codes.astype(jnp.float32)
    weights = 2.5 * codes_float / jnp.sum(codes_float, axis=1, keepdims=True)
    projected = projected.reshape(token_count, pick_count, rank_width)
    return jnp.sum(weights[:, :, None] * projected, axis=1).astype(jnp.bfloat16)


def solution(mesh):
    in_specs = (
        P(("group", "expert"), None),
        P(("group", "expert"), None),
        P(("group", "expert"), None),
        P("expert", None, None),
        P("expert", None, None),
        P("expert", None, None),
        P("expert", None),
    )
    out_specs = P(("group", "expert"), None)
    return jax.shard_map(shards, mesh=mesh, in_specs=in_specs, out_specs=out_specs, check_vma=False)
```

profile of v0, /device:TPU:0, one launch (start us, length us, event | category | flops | bytes accessed | tf_op | source)
XLA Modules:
  0.0 121.8 jit_solution(8186890199680378276)
XLA Ops:
  6.5 0.0 copy-start
  6.5 0.0 all-gather.2.cloned.1.call-start
  6.5 0.7 all-gather.2.cloned.1.call-update
  7.3 0.8 copy.25
  8.0 0.1 eq.15
  8.1 0.7 broadcast_multiply_fusion
  8.8 0.1 copy.24
  8.9 0.1 mul.37
  9.0 0.2 reduce_window_sum.11
  9.2 0.8 concatenate.3
  10.1 0.6 scatter_custom_fusion
  10.7 0.6 gather_fusion
  11.3 0.1 broadcast_in_dim.7
  11.4 1.2 broadcast_in_dim.8
  12.5 7.4 %all-to-all-start = ((bf16[16,4,7168]{2,1,0:T(4,128)(2,1)}), bf16[16,4,7168]{2,1,0:T(4,128)(2,1)S(1)}, u32[]{:S(2)}, u32[]{:S(2)}) async-start(bf16[16,4,7168]{2,1,0:T(4,128)(2,1)} %bitcast.2), calls=%async_computation | async-start | bytes 1835008 | tf_op jit(solution)/shard_map/all_to_all | solution.py:45
  19.9 0.0 copy-done
  20.0 35.1 %all-to-all-done = bf16[16,4,7168]{2,1,0:T(4,128)(2,1)S(1)} async-done(((bf16[16,4,7168]{2,1,0:T(4,128)(2,1)}), bf16[16,4,7168]{2,1,0:T(4,128)(2,1)S(1)}, u32[]{:S(2)}, u32[]{:S(2)}) %all-to-all-start) | async-done | bytes 917536 | tf_op jit(solution)/shard_map/all_to_all | solution.py:45
  55.1 0.2 reshape.53
  55.3 2.8 %fusion.5 = f32[64,256]{1,0:T(8,128)S(1)} fusion(bf16[64,7168]{1,0:T(8,128)(2,1)S(1)} %reshape.53, bf16[1,7168,256]{2,1,0:T(8,128)(2,1)} %param.10), kind=kOutput, calls=%fused_computation.9 | convolution fusion | flops 234881024 | bytes 4653056 | tf_op jit(solution)/shard_map/dot_general | solution.py:12
  58.0 5.5 %convolution_convert_fusion = bf16[64,7168]{1,0:T(8,128)(2,1)S(1)} fusion(bf16[1,256,7168]{2,1,0:T(8,128)(2,1)} %param.12, bf16[64,7168]{1,0:T(8,128)(2,1)S(1)} %reshape.53, bf16[1,7168,256]{2,1,0:T(8,128)(2,1)} %param.11, f32[64,256]{1,0:T(8,128)S(1)} %fusion.5), kind=kOutput, calls=%fused_computation.3 | convolution fusion | flops 470319104 | bytes 9240576 | tf_op jit(solution)/shard_map/dot_general | solution.py:15
  63.5 0.3 reshape.54
  63.8 33.4 %all-gather.2.cloned.1.call-done = bf16[7168,512]{1,0:T(8,128)(2,1)} async-done(((bf16[448,512]{1,0:T(8,128)(2,1)}), bf16[7168,512]{1,0:T(8,128)(2,1)}) %all-gather.2.cloned.1.call-update) | async-done | bytes 7340048 | tf_op jit(solution)/shard_map/all_gather | solution.py:43
  97.3 4.2 %fusion = f32[16,4,512]{2,0,1:T(8,128)S(1)} fusion(bf16[7168,512]{1,0:T(8,128)(2,1)} %all-gather.2.cloned.1.call-done, bf16[16,4,7168]{2,1,0:T(4,128)(2,1)S(1)} %reshape.54), kind=kOutput, calls=%fused_computation.4 | convolution fusion | flops 469762048 | bytes 8388608 | tf_op jit(solution)/shard_map/skd,dr->skr/dot_general | solution.py:50
  101.5 0.7 copy.27
  102.2 3.5 %all-to-all-start.1 = ((f32[16,4,512]{2,1,0:T(4,128)}), f32[16,4,512]{2,1,0:T(4,128)S(1)}, u32[]{:S(2)}, u32[]{:S(2)}) async-start(f32[16,4,512]{2,1,0:T(4,128)} %copy.27), calls=%async_computation.1 | async-start | bytes 262144 | tf_op jit(solution)/shard_map/all_to_all | solution.py:51
  105.8 0.1 copy.23
  105.9 7.8 %all-to-all-done.1 = f32[16,4,512]{2,1,0:T(4,128)S(1)} async-done(((f32[16,4,512]{2,1,0:T(4,128)}), f32[16,4,512]{2,1,0:T(4,128)S(1)}, u32[]{:S(2)}, u32[]{:S(2)}) %all-to-all-start.1) | async-done | bytes 131104 | tf_op jit(solution)/shard_map/all_to_all | solution.py:51
  113.7 0.6 gather_fusion.1
  114.2 0.7 multiply_reduce_fusion
  (12 shorter events, 0.1 us)
Async XLA Ops:
  6.5 13.4 %copy-start = (s32[4,2]{0,1:T(2,128)S(1)}, s32[4,2]{0,1:T(2,128)}, u32[]{:S(2)}) copy-start(s32[4,2]{0,1:T(2,128)} %param.9) | copy-start | bytes 100
  6.5 90.7 %all-gather.2.cloned.1.call-start = ((), (), s32[]{:S(2)}) async-start(), calls=%async_computation.2 | async-start | bytes 7798784 | tf_op jit(solution)/shard_map/all_gather | solution.py:43
  12.5 42.5 %all-to-all-start = ((bf16[16,4,7168]{2,1,0:T(4,128)(2,1)}), bf16[16,4,7168]{2,1,0:T(4,128)(2,1)S(1)}, u32[]{:S(2)}, u32[]{:S(2)}) async-start(bf16[16,4,7168]{2,1,0:T(4,128)(2,1)} %bitcast.2), calls=%async_computation | async-start | bytes 1835008 | tf_op jit(solution)/shard_map/all_to_all | solution.py:45
  102.2 11.4 %all-to-all-start.1 = ((f32[16,4,512]{2,1,0:T(4,128)}), f32[16,4,512]{2,1,0:T(4,128)S(1)}, u32[]{:S(2)}, u32[]{:S(2)}) async-start(f32[16,4,512]{2,1,0:T(4,128)} %copy.27), calls=%async_computation.1 | async-start | bytes 262144 | tf_op jit(solution)/shard_map/all_to_all | solution.py:51
Sparse Core Ops, SparseCore 0:
  9.6 87.5 all-gather.1
where the time goes:
time: 122 us
  waiting for transfers between devices  77 us (63%)
  between operations  13.5 us (11%)
  matrix products  12.4 us (10%)
  starting transfers between devices  10.9 us (9%)
  local copies, waits for them, and re-layouts  6.25 us (5%)
  other arithmetic  1.66 us (1%)
    all_to_all x1, waiting for transfers between devices, shards(): lax.all_to_all(outgoing, 'expert', split_axis=0, concat_axis=0, tiled=True)  35.1 us
    all_gather x1, waiting for transfers between devices, shards(): full_basis = lax.all_gather(target_basis, 'expert', axis=0, tiled=True)  33.4 us
    all_to_all x1, waiting for transfers between devices, shards(): lax.all_to_all(result, 'expert', split_axis=0, concat_axis=0, tiled=True)  7.76 us
    all_to_all x1, starting transfers between devices, shards(): lax.all_to_all(outgoing, 'expert', split_axis=0, concat_axis=0, tiled=True)  7.41 us
    dot_general x1, matrix products, run_expert(): jnp.dot(hidden, down_weight[0], preferred_element_type=jnp.float32)  5.45 us
    dot_general x1, matrix products, shards(): jnp.einsum('skd,dr->skr', expert_part, full_basis, preferred_element_type...  4.23 us
    all_to_all x1, starting transfers between devices, shards(): lax.all_to_all(result, 'expert', split_axis=0, concat_axis=0, tiled=True)  3.51 us
    dot_general x1, matrix products, run_expert(): jnp.dot(row_block, gate_weight[0], preferred_element_type=jnp.float32)  2.76 us
  transfers between devices with their start and end apart: 3, of which 3 were waited for; matrix products, arithmetic and copies ran while one was open for 12% of the time, Pallas kernels for 0%

commit v1 on v0

--- a/solution.py
+++ b/solution.py
@@ -4,6 +4,22 @@
 from jax.sharding import PartitionSpec as P
 
 SLICES = 8
+
+
+def summed_both_ways(value, axis, dim, product):
+    size, index, width = (lax.axis_size(axis), lax.axis_index(axis), value.shape[dim])
+    upward = [(i, (i + 1) % size) for i in range(size)]
+    backward = [(i, (i - 1) % size) for i in range(size)]
+    half = size // 2
+    from_left = from_right = value
+    total = product(value, index * width)
+    for turn in range(1, half + 1):
+        from_left = lax.ppermute(from_left, axis, upward)
+        if turn < size - half:
+            from_right = lax.ppermute(from_right, axis, backward)
+            total = total + product(from_right, (index + turn) % size * width)
+        total = total + product(from_left, (index - turn) % size * width)
+    return total
 
 
 def run_expert(received, gate_weight, up_weight, down_weight):
@@ -40,14 +56,23 @@
     per_expert_rows = padded[slot_table].reshape(expert_count, 1, capacity, feature_width)
     outgoing = jnp.broadcast_to(per_expert_rows, (expert_count, SLICES, capacity, feature_width))
     outgoing = outgoing.reshape(owner_count, capacity, feature_width)
-    full_basis = lax.all_gather(target_basis, "expert", axis=0, tiled=True)
     expert_part = run_expert(
         lax.all_to_all(outgoing, "expert", split_axis=0, concat_axis=0, tiled=True),
         gate_weight,
         up_weight,
         down_weight,
     )
-    result = jnp.einsum("skd,dr->skr", expert_part, full_basis, preferred_element_type=jnp.float32)
+    result = summed_both_ways(
+        target_basis,
+        "expert",
+        0,
+        lambda shard, start: jnp.einsum(
+            "skd,dr->skr",
+            lax.dynamic_slice_in_dim(expert_part, start, shard.shape[0], axis=2),
+            shard,
+            preferred_element_type=jnp.float32,
+        ),
+    )
     returned = lax.all_to_all(result, "expert", split_axis=0, concat_axis=0, tiled=True)
     summed = jnp.sum(returned.reshape(expert_count, SLICES, capacity, rank_width), axis=1)
     projected = summed.reshape(expert_count * capacity, rank_width)[slot_index]

time: 122 us -> 144 us (1.18)
  starting transfers between devices: 10.9 us -> 50.7 us
  between operations: 13.5 us -> 0.35 us
  waiting for transfers between devices: 77 us -> 67.2 us
  matrix products: 12.4 us -> 16.4 us
    ppermute x0 -> x15, waiting for transfers between devices: none -> 59.4 us  [the longest x8 59.4 us: summed_both_ways(): from_left = lax.ppermute(from_left, axis, upward)]
    all_to_all x1, waiting for transfers between devices: 35.1 us -> 0.01 us  [shards(): lax.all_to_all(outgoing, 'expert', split_axis=0, concat_axis=0, tiled=True)]
    all_gather x1 -> x0, waiting for transfers between devices: 33.4 us -> none  [shards(): full_basis = lax.all_gather(target_basis, 'expert', axis=0, tiled=True)]
    ppermute x0 -> x15, starting transfers between devices: none -> 31.7 us  [the longest x7 31.1 us: summed_both_ways(): from_right = lax.ppermute(from_right, axis, backward)]
    all_to_all x1, starting transfers between devices: 3.51 us -> 11.6 us  [shards(): lax.all_to_all(result, 'expert', split_axis=0, concat_axis=0, tiled=True)]
    dot_general x1 -> x16, matrix products: 4.23 us -> 8.21 us  [shards(): jnp.einsum('skd,dr->skr', lax.dynamic_slice_in_dim(expert_part, start, sh...]
  transfers between devices with their start and end apart: 3 -> 17, of which waited for: 3 -> 9; matrix products, arithmetic and copies ran while one was open for 12% -> 13% of each run, Pallas kernels for 0% -> 0%
where the time goes in v1:
time: 144 us
  waiting for transfers between devices  67.2 us (47%)
  starting transfers between devices  50.7 us (35%)
  matrix products  16.4 us (11%)
  local copies, waits for them, and re-layouts  7.57 us (5%)
  other arithmetic  1.66 us (1%)
    ppermute x8, waiting for transfers between devices, summed_both_ways(): from_left = lax.ppermute(from_left, axis, upward)  59.4 us
    ppermute x7, starting transfers between devices, summed_both_ways(): from_right = lax.ppermute(from_right, axis, backward)  31.1 us
    all_to_all x1, starting transfers between devices, shards(): lax.all_to_all(result, 'expert', split_axis=0, concat_axis=0, tiled=True)  11.6 us
    dot_general x16, matrix products, shards(): jnp.einsum('skd,dr->skr', lax.dynamic_slice_in_dim(expert_part, start, sh...  8.21 us
    all_to_all x1, waiting for transfers between devices, shards(): lax.all_to_all(result, 'expert', split_axis=0, concat_axis=0, tiled=True)  7.79 us
    all_to_all x1, starting transfers between devices, shards(): lax.all_to_all(outgoing, 'expert', split_axis=0, concat_axis=0, tiled=True)  7.41 us
    dot_general x1, matrix products, run_expert(): jnp.dot(hidden, down_weight[0], preferred_element_type=jnp.float32)  5.45 us
  transfers between devices with their start and end apart: 17, of which 9 were waited for; matrix products, arithmetic and copies ran while one was open for 13% of the time, Pallas kernels for 0%

profile of v1, /device:TPU:0, one launch (start us, length us, event | category | flops | bytes accessed | tf_op | source)
XLA Modules:
  0.0 143.9 jit_solution(13761975763164862819)
XLA Ops:
  0.0 0.8 copy.70
  0.8 0.7 broadcast_multiply_fusion
  2.0 0.6 scatter_custom_fusion
  2.6 0.8 concatenate.3
  3.5 0.6 gather_fusion
  4.2 1.2 broadcast_in_dim.8
  5.3 7.4 %all-to-all-start = ((bf16[16,4,7168]{2,1,0:T(4,128)(2,1)}), bf16[16,4,7168]{2,1,0:T(4,128)(2,1)S(1)}, u32[]{:S(2)}, u32[]{:S(2)}) async-start(bf16[16,4,7168]{2,1,0:T(4,128)(2,1)} %bitcast.2), calls=%async_computation | async-start | bytes 1835008 | tf_op jit(solution)/shard_map/all_to_all | solution.py:60
  12.7 0.5 collective-permute-start.1
  13.2 4.0 %collective-permute-start = (bf16[448,512]{1,0:T(8,128)(2,1)S(1)}, bf16[448,512]{1,0:T(8,128)(2,1)}, u32[]{:S(2)}, u32[]{:S(2)}) collective-permute-start(bf16[448,512]{1,0:T(8,128)(2,1)S(1)} %copy-done), channel_id=1, source_target_pairs={{0,15},{1,0},{2,1},{3,2},{4,3},{5,4},{6,5},{7,6},{8,7},{9,8},{10,9... | collective-permute-start | bytes 1376264 | tf_op jit(solution)/shard_map/ppermute | solution.py:19
  17.2 21.3 %collective-permute-done.1 = bf16[448,512]{1,0:T(8,128)(2,1)S(1)} collective-permute-done((bf16[448,512]{1,0:T(8,128)(2,1)S(1)}, bf16[448,512]{1,0:T(8,128)(2,1)S(1)}, u32[]{:S(2)}, u32[]{:S(2)}) %collective-permute-start.1) | collective-permute-done | bytes 458784 | tf_op jit(solution)/shard_map/ppermute | solution.py:17
  38.5 4.4 %collective-permute-start.2 = (bf16[448,512]{1,0:T(8,128)(2,1)}, bf16[448,512]{1,0:T(8,128)(2,1)S(1)}, u32[]{:S(2)}, u32[]{:S(2)}) collective-permute-start(bf16[448,512]{1,0:T(8,128)(2,1)} %collective-permute-done), channel_id=1, source_target_pairs={{0,15},{1,0},{2,1},{3,2},{4,3},{5,4},{6,5},{7,6},{8,7},{9,8},{10,9... | collective-permute-start | bytes 1376264 | tf_op jit(solution)/shard_map/ppermute | solution.py:19
  43.0 6.3 %collective-permute-done.3 = bf16[448,512]{1,0:T(8,128)(2,1)S(1)} collective-permute-done((bf16[448,512]{1,0:T(8,128)(2,1)S(1)}, bf16[448,512]{1,0:T(8,128)(2,1)S(1)}, u32[]{:S(2)}, u32[]{:S(2)}) %collective-permute-start.3) | collective-permute-done | bytes 458784 | tf_op jit(solution)/shard_map/ppermute | solution.py:17
  49.3 4.6 %collective-permute-start.4 = (bf16[448,512]{1,0:T(8,128)(2,1)S(1)}, bf16[448,512]{1,0:T(8,128)(2,1)}, u32[]{:S(2)}, u32[]{:S(2)}) collective-permute-start(bf16[448,512]{1,0:T(8,128)(2,1)S(1)} %collective-permute-done.2), channel_id=1, source_target_pairs={{0,15},{1,0},{2,1},{3,2},{4,3},{5,4},{6,5},{7,6},{8,7},{9,8},{10,9... | collective-permute-start | bytes 1376264 | tf_op jit(solution)/shard_map/ppermute | solution.py:19
  53.9 6.0 %collective-permute-done.5 = bf16[448,512]{1,0:T(8,128)(2,1)} collective-permute-done((bf16[448,512]{1,0:T(8,128)(2,1)S(1)}, bf16[448,512]{1,0:T(8,128)(2,1)}, u32[]{:S(2)}, u32[]{:S(2)}) %collective-permute-start.5) | collective-permute-done | bytes 458784 | tf_op jit(solution)/shard_map/ppermute | solution.py:17
  60.0 4.8 %collective-permute-start.6 = (bf16[448,512]{1,0:T(8,128)(2,1)}, bf16[448,512]{1,0:T(8,128)(2,1)}, u32[]{:S(2)}, u32[]{:S(2)}) collective-permute-start(bf16[448,512]{1,0:T(8,128)(2,1)} %collective-permute-done.4), channel_id=1, source_target_pairs={{0,15},{1,0},{2,1},{3,2},{4,3},{5,4},{6,5},{7,6},{8,7},{9,8},{10,9... | collective-permute-start | bytes 1376264 | tf_op jit(solution)/shard_map/ppermute | solution.py:19
  64.7 0.2 reshape.53
  64.9 2.8 %fusion.3 = f32[64,256]{1,0:T(8,128)S(1)} fusion(bf16[64,7168]{1,0:T(8,128)(2,1)S(1)} %reshape.53, bf16[1,7168,256]{2,1,0:T(8,128)(2,1)} %param.10), kind=kOutput, calls=%fused_computation.7 | convolution fusion | flops 234881024 | bytes 4653056 | tf_op jit(solution)/shard_map/dot_general | solution.py:28
  67.7 5.5 %convolution_convert_fusion = bf16[64,7168]{1,0:T(8,128)(2,1)S(1)} fusion(bf16[1,256,7168]{2,1,0:T(8,128)(2,1)} %param.12, bf16[64,7168]{1,0:T(8,128)(2,1)S(1)} %reshape.53, bf16[1,7168,256]{2,1,0:T(8,128)(2,1)} %param.11, f32[64,256]{1,0:T(8,128)S(1)} %fusion.3), kind=kOutput, calls=%fused_computation.3 | convolution fusion | flops 470319104 | bytes 9240576 | tf_op jit(solution)/shard_map/dot_general | solution.py:31
  73.2 0.3 reshape.54
  73.5 1.2 constant_dynamic-slice_fusion
  74.8 0.2 fusion.40
  75.0 0.2 fusion.35
  75.2 1.2 convolution_add_fusion.8
  76.4 0.2 convolution_add_fusion.7
  76.6 0.2 fusion.10
  76.8 1.2 fusion.32
  78.0 1.2 fusion.9
  79.4 4.4 %collective-permute-start.8 = (bf16[448,512]{1,0:T(8,128)(2,1)}, bf16[448,512]{1,0:T(8,128)(2,1)S(1)}, u32[]{:S(2)}, u32[]{:S(2)}) collective-permute-start(bf16[448,512]{1,0:T(8,128)(2,1)} %collective-permute-done.6), channel_id=1, source_target_pairs={{0,15},{1,0},{2,1},{3,2},{4,3},{5,4},{6,5},{7,6},{8,7},{9,8},{10,9... | collective-permute-start | bytes 1376264 | tf_op jit(solution)/shard_map/ppermute | solution.py:19
  83.8 1.2 fusion.29
  85.0 1.2 fusion.8
  86.2 4.0 %collective-permute-done.9 = bf16[448,512]{1,0:T(8,128)(2,1)S(1)} collective-permute-done((bf16[448,512]{1,0:T(8,128)(2,1)}, bf16[448,512]{1,0:T(8,128)(2,1)S(1)}, u32[]{:S(2)}, u32[]{:S(2)}) %collective-permute-start.9) | collective-permute-done | bytes 458784 | tf_op jit(solution)/shard_map/ppermute | solution.py:17
  90.2 4.4 %collective-permute-start.10 = (bf16[448,512]{1,0:T(8,128)(2,1)S(1)}, bf16[448,512]{1,0:T(8,128)(2,1)S(1)}, u32[]{:S(2)}, u32[]{:S(2)}) collective-permute-start(bf16[448,512]{1,0:T(8,128)(2,1)S(1)} %collective-permute-done.8), channel_id=1, source_target_pairs={{0,15},{1,0},{2,1},{3,2},{4,3},{5,4},{6,5},{7,6},{8,7},{9,8},{10,9... | collective-permute-start | bytes 1376264 | tf_op jit(solution)/shard_map/ppermute | solution.py:19
  94.7 0.2 fusion.26
  94.9 0.2 fusion.7
  95.1 5.8 %collective-permute-done.11 = bf16[448,512]{1,0:T(8,128)(2,1)S(1)} collective-permute-done((bf16[448,512]{1,0:T(8,128)(2,1)S(1)}, bf16[448,512]{1,0:T(8,128)(2,1)S(1)}, u32[]{:S(2)}, u32[]{:S(2)}) %collective-permute-start.11) | collective-permute-done | bytes 458784 | tf_op jit(solution)/shard_map/ppermute | solution.py:17
  101.0 4.4 %collective-permute-start.12 = (bf16[448,512]{1,0:T(8,128)(2,1)S(1)}, bf16[448,512]{1,0:T(8,128)(2,1)S(1)}, u32[]{:S(2)}, u32[]{:S(2)}) collective-permute-start(bf16[448,512]{1,0:T(8,128)(2,1)S(1)} %collective-permute-done.10), channel_id=1, source_target_pairs={{0,15},{1,0},{2,1},{3,2},{4,3},{5,4},{6,5},{7,6},{8,7},{9,8},{10,9... | collective-permute-start | bytes 1376264 | tf_op jit(solution)/shard_map/ppermute | solution.py:19
  105.4 0.2 fusion.23
  105.6 0.2 fusion.6
  105.8 5.7 %collective-permute-done.13 = bf16[448,512]{1,0:T(8,128)(2,1)S(1)} collective-permute-done((bf16[448,512]{1,0:T(8,128)(2,1)S(1)}, bf16[448,512]{1,0:T(8,128)(2,1)S(1)}, u32[]{:S(2)}, u32[]{:S(2)}) %collective-permute-start.13) | collective-permute-done | bytes 458784 | tf_op jit(solution)/shard_map/ppermute | solution.py:17
  111.5 0.2 fusion.20
  111.8 0.2 fusion.5
  112.0 10.2 %collective-permute-done.14 = bf16[448,512]{1,0:T(8,128)(2,1)S(1)} collective-permute-done((bf16[448,512]{1,0:T(8,128)(2,1)S(1)}, bf16[448,512]{1,0:T(8,128)(2,1)S(1)}, u32[]{:S(2)}, u32[]{:S(2)}) %collective-permute-start.14) | collective-permute-done | bytes 458784 | tf_op jit(solution)/shard_map/ppermute | solution.py:17
  122.1 0.2 convolution_add_fusion
  122.3 0.7 copy.87
  123.1 11.6 %all-to-all-start.1 = ((f32[16,4,512]{2,1,0:T(4,128)}), f32[16,4,512]{2,1,0:T(4,128)S(1)}, u32[]{:S(2)}, u32[]{:S(2)}) async-start(f32[16,4,512]{2,1,0:T(4,128)} %copy.87), calls=%async_computation.1 | async-start | bytes 262144 | tf_op jit(solution)/shard_map/all_to_all | solution.py:76
  134.8 7.8 %all-to-all-done.1 = f32[16,4,512]{2,1,0:T(4,128)S(1)} async-done(((f32[16,4,512]{2,1,0:T(4,128)}), f32[16,4,512]{2,1,0:T(4,128)S(1)}, u32[]{:S(2)}, u32[]{:S(2)}) %all-to-all-start.1) | async-done | bytes 131104 | tf_op jit(solution)/shard_map/all_to_all | solution.py:76
  142.6 0.6 gather_fusion.1
  143.2 0.7 multiply_reduce_fusion
  (50 shorter events, 0.9 us)
Async XLA Ops:
  0.0 12.7 %copy-start = (bf16[448,512]{1,0:T(8,128)(2,1)S(1)}, bf16[448,512]{1,0:T(8,128)(2,1)}, u32[]{:S(2)}) copy-start(bf16[448,512]{1,0:T(8,128)(2,1)} %param.13) | copy-start | bytes 1376260
  0.0 53.9 %copy-start.7 = (s32[4,2]{0,1:T(2,128)S(1)}, s32[4,2]{0,1:T(2,128)}, u32[]{:S(2)}) copy-start(s32[4,2]{0,1:T(2,128)} %param.9) | copy-start | bytes 100
  5.3 59.4 %all-to-all-start = ((bf16[16,4,7168]{2,1,0:T(4,128)(2,1)}), bf16[16,4,7168]{2,1,0:T(4,128)(2,1)S(1)}, u32[]{:S(2)}, u32[]{:S(2)}) async-start(bf16[16,4,7168]{2,1,0:T(4,128)(2,1)} %bitcast.2), calls=%async_computation | async-start | bytes 1835008 | tf_op jit(solution)/shard_map/all_to_all | solution.py:60
  12.7 25.8 %collective-permute-start.1 = (bf16[448,512]{1,0:T(8,128)(2,1)S(1)}, bf16[448,512]{1,0:T(8,128)(2,1)S(1)}, u32[]{:S(2)}, u32[]{:S(2)}) collective-permute-start(bf16[448,512]{1,0:T(8,128)(2,1)S(1)} %copy-done), channel_id=1, source_target_pairs={{0,1},{1,2},{2,3},{3,4},{4,5},{5,6},{6,7},{7,8},{8,9},{9,10},{10,1... | collective-permute-start | bytes 1376264 | tf_op jit(solution)/shard_map/ppermute | solution.py:17
  13.2 25.3 %collective-permute-start = (bf16[448,512]{1,0:T(8,128)(2,1)S(1)}, bf16[448,512]{1,0:T(8,128)(2,1)}, u32[]{:S(2)}, u32[]{:S(2)}) collective-permute-start(bf16[448,512]{1,0:T(8,128)(2,1)S(1)} %copy-done), channel_id=1, source_target_pairs={{0,15},{1,0},{2,1},{3,2},{4,3},{5,4},{6,5},{7,6},{8,7},{9,8},{10,9... | collective-permute-start | bytes 1376264 | tf_op jit(solution)/shard_map/ppermute | solution.py:19
  38.5 26.4 %copy-start.5 = (bf16[448,512]{1,0:T(8,128)(2,1)}, bf16[448,512]{1,0:T(8,128)(2,1)S(1)}, u32[]{:S(2)}) copy-start(bf16[448,512]{1,0:T(8,128)(2,1)S(1)} %collective-permute-done.1) | copy-start | bytes 1376260
  38.5 10.7 %collective-permute-start.3 = (bf16[448,512]{1,0:T(8,128)(2,1)S(1)}, bf16[448,512]{1,0:T(8,128)(2,1)S(1)}, u32[]{:S(2)}, u32[]{:S(2)}) collective-permute-start(bf16[448,512]{1,0:T(8,128)(2,1)S(1)} %collective-permute-done.1), channel_id=1, source_target_pairs={{0,1},{1,2},{2,3},{3,4},{4,5},{5,6},{6,7},{7,8},{8,9},{9,10},{10,1... | collective-permute-start | bytes 1376264 | tf_op jit(solution)/shard_map/ppermute | solution.py:17
  38.5 10.8 %collective-permute-start.2 = (bf16[448,512]{1,0:T(8,128)(2,1)}, bf16[448,512]{1,0:T(8,128)(2,1)S(1)}, u32[]{:S(2)}, u32[]{:S(2)}) collective-permute-start(bf16[448,512]{1,0:T(8,128)(2,1)} %collective-permute-done), channel_id=1, source_target_pairs={{0,15},{1,0},{2,1},{3,2},{4,3},{5,4},{6,5},{7,6},{8,7},{9,8},{10,9... | collective-permute-start | bytes 1376264 | tf_op jit(solution)/shard_map/ppermute | solution.py:19
  49.2 15.5 %copy-start.3 = (bf16[448,512]{1,0:T(8,128)(2,1)}, bf16[448,512]{1,0:T(8,128)(2,1)S(1)}, u32[]{:S(2)}) copy-start(bf16[448,512]{1,0:T(8,128)(2,1)S(1)} %collective-permute-done.3) | copy-start | bytes 1376260
  49.2 10.7 %collective-permute-start.5 = (bf16[448,512]{1,0:T(8,128)(2,1)S(1)}, bf16[448,512]{1,0:T(8,128)(2,1)}, u32[]{:S(2)}, u32[]{:S(2)}) collective-permute-start(bf16[448,512]{1,0:T(8,128)(2,1)S(1)} %collective-permute-done.3), channel_id=1, source_target_pairs={{0,1},{1,2},{2,3},{3,4},{4,5},{5,6},{6,7},{7,8},{8,9},{9,10},{10,1... | collective-permute-start | bytes 1376264 | tf_op jit(solution)/shard_map/ppermute | solution.py:17
  49.3 15.4 %copy-start.1 = (bf16[448,512]{1,0:T(8,128)(2,1)}, bf16[448,512]{1,0:T(8,128)(2,1)S(1)}, u32[]{:S(2)}) copy-start(bf16[448,512]{1,0:T(8,128)(2,1)S(1)} %collective-permute-done.2) | copy-start | bytes 1376260
  49.3 10.7 %collective-permute-start.4 = (bf16[448,512]{1,0:T(8,128)(2,1)S(1)}, bf16[448,512]{1,0:T(8,128)(2,1)}, u32[]{:S(2)}, u32[]{:S(2)}) collective-permute-start(bf16[448,512]{1,0:T(8,128)(2,1)S(1)} %collective-permute-done.2), channel_id=1, source_target_pairs={{0,15},{1,0},{2,1},{3,2},{4,3},{5,4},{6,5},{7,6},{8,7},{9,8},{10,9... | collective-permute-start | bytes 1376264 | tf_op jit(solution)/shard_map/ppermute | solution.py:19
  59.9 19.3 %collective-permute-start.7 = (bf16[448,512]{1,0:T(8,128)(2,1)}, bf16[448,512]{1,0:T(8,128)(2,1)}, u32[]{:S(2)}, u32[]{:S(2)}) collective-permute-start(bf16[448,512]{1,0:T(8,128)(2,1)} %collective-permute-done.5), channel_id=1, source_target_pairs={{0,1},{1,2},{2,3},{3,4},{4,5},{5,6},{6,7},{7,8},{8,9},{9,10},{10,1... | collective-permute-start | bytes 1376264 | tf_op jit(solution)/shard_map/ppermute | solution.py:17
  60.0 19.4 %collective-permute-start.6 = (bf16[448,512]{1,0:T(8,128)(2,1)}, bf16[448,512]{1,0:T(8,128)(2,1)}, u32[]{:S(2)}, u32[]{:S(2)}) collective-permute-start(bf16[448,512]{1,0:T(8,128)(2,1)} %collective-permute-done.4), channel_id=1, source_target_pairs={{0,15},{1,0},{2,1},{3,2},{4,3},{5,4},{6,5},{7,6},{8,7},{9,8},{10,9... | collective-permute-start | bytes 1376264 | tf_op jit(solution)/shard_map/ppermute | solution.py:19
  73.2 1.8 %copy-start.4 = (bf16[448,512]{1,0:T(8,128)(2,1)S(1)}, bf16[448,512]{1,0:T(8,128)(2,1)}, u32[]{:S(2)}) copy-start(bf16[448,512]{1,0:T(8,128)(2,1)} %copy-done.3) | copy-start | bytes 1376260
  73.2 3.4 %copy-start.2 = (bf16[448,512]{1,0:T(8,128)(2,1)S(1)}, bf16[448,512]{1,0:T(8,128)(2,1)}, u32[]{:S(2)}) copy-start(bf16[448,512]{1,0:T(8,128)(2,1)} %copy-done.1) | copy-start | bytes 1376260
  73.5 2.9 %copy-start.6 = (bf16[448,512]{1,0:T(8,128)(2,1)S(1)}, bf16[448,512]{1,0:T(8,128)(2,1)}, u32[]{:S(2)}) copy-start(bf16[448,512]{1,0:T(8,128)(2,1)} %copy-done.5) | copy-start | bytes 1376260
  79.3 11.0 %collective-permute-start.9 = (bf16[448,512]{1,0:T(8,128)(2,1)}, bf16[448,512]{1,0:T(8,128)(2,1)S(1)}, u32[]{:S(2)}, u32[]{:S(2)}) collective-permute-start(bf16[448,512]{1,0:T(8,128)(2,1)} %collective-permute-done.7), channel_id=1, source_target_pairs={{0,1},{1,2},{2,3},{3,4},{4,5},{5,6},{6,7},{7,8},{8,9},{9,10},{10,1... | collective-permute-start | bytes 1376264 | tf_op jit(solution)/shard_map/ppermute | solution.py:17
  79.4 10.9 %collective-permute-start.8 = (bf16[448,512]{1,0:T(8,128)(2,1)}, bf16[448,512]{1,0:T(8,128)(2,1)S(1)}, u32[]{:S(2)}, u32[]{:S(2)}) collective-permute-start(bf16[448,512]{1,0:T(8,128)(2,1)} %collective-permute-done.6), channel_id=1, source_target_pairs={{0,15},{1,0},{2,1},{3,2},{4,3},{5,4},{6,5},{7,6},{8,7},{9,8},{10,9... | collective-permute-start | bytes 1376264 | tf_op jit(solution)/shard_map/ppermute | solution.py:19
  90.2 10.7 %collective-permute-start.11 = (bf16[448,512]{1,0:T(8,128)(2,1)S(1)}, bf16[448,512]{1,0:T(8,128)(2,1)S(1)}, u32[]{:S(2)}, u32[]{:S(2)}) collective-permute-start(bf16[448,512]{1,0:T(8,128)(2,1)S(1)} %collective-permute-done.9), channel_id=1, source_target_pairs={{0,1},{1,2},{2,3},{3,4},{4,5},{5,6},{6,7},{7,8},{8,9},{9,10},{10,1... | collective-permute-start | bytes 1376264 | tf_op jit(solution)/shard_map/ppermute | solution.py:17
  90.2 10.7 %collective-permute-start.10 = (bf16[448,512]{1,0:T(8,128)(2,1)S(1)}, bf16[448,512]{1,0:T(8,128)(2,1)S(1)}, u32[]{:S(2)}, u32[]{:S(2)}) collective-permute-start(bf16[448,512]{1,0:T(8,128)(2,1)S(1)} %collective-permute-done.8), channel_id=1, source_target_pairs={{0,15},{1,0},{2,1},{3,2},{4,3},{5,4},{6,5},{7,6},{8,7},{9,8},{10,9... | collective-permute-start | bytes 1376264 | tf_op jit(solution)/shard_map/ppermute | solution.py:19
  100.9 10.6 %collective-permute-start.13 = (bf16[448,512]{1,0:T(8,128)(2,1)S(1)}, bf16[448,512]{1,0:T(8,128)(2,1)S(1)}, u32[]{:S(2)}, u32[]{:S(2)}) collective-permute-start(bf16[448,512]{1,0:T(8,128)(2,1)S(1)} %collective-permute-done.11), channel_id=1, source_target_pairs={{0,1},{1,2},{2,3},{3,4},{4,5},{5,6},{6,7},{7,8},{8,9},{9,10},{10,1... | collective-permute-start | bytes 1376264 | tf_op jit(solution)/shard_map/ppermute | solution.py:17
  101.0 10.8 %collective-permute-start.12 = (bf16[448,512]{1,0:T(8,128)(2,1)S(1)}, bf16[448,512]{1,0:T(8,128)(2,1)S(1)}, u32[]{:S(2)}, u32[]{:S(2)}) collective-permute-start(bf16[448,512]{1,0:T(8,128)(2,1)S(1)} %collective-permute-done.10), channel_id=1, source_target_pairs={{0,15},{1,0},{2,1},{3,2},{4,3},{5,4},{6,5},{7,6},{8,7},{9,8},{10,9... | collective-permute-start | bytes 1376264 | tf_op jit(solution)/shard_map/ppermute | solution.py:19
  111.5 10.6 %collective-permute-start.14 = (bf16[448,512]{1,0:T(8,128)(2,1)S(1)}, bf16[448,512]{1,0:T(8,128)(2,1)S(1)}, u32[]{:S(2)}, u32[]{:S(2)}) collective-permute-start(bf16[448,512]{1,0:T(8,128)(2,1)S(1)} %collective-permute-done.13), channel_id=1, source_target_pairs={{0,1},{1,2},{2,3},{3,4},{4,5},{5,6},{6,7},{7,8},{8,9},{9,10},{10,1... | collective-permute-start | bytes 1376264 | tf_op jit(solution)/shard_map/ppermute | solution.py:17
  123.1 19.5 %all-to-all-start.1 = ((f32[16,4,512]{2,1,0:T(4,128)}), f32[16,4,512]{2,1,0:T(4,128)S(1)}, u32[]{:S(2)}, u32[]{:S(2)}) async-start(f32[16,4,512]{2,1,0:T(4,128)} %copy.87), calls=%async_computation.1 | async-start | bytes 262144 | tf_op jit(solution)/shard_map/all_to_all | solution.py:76
